TPU v7x, 32 devices: a whole 2x2x4 slice. The times are simulated.
32 devices in a mesh: band: 4 (over y, x), query: 8 (over z, core).
Axes of the slice: x: 2, y: 2, z: 4, core: 2. Of those that a mesh axis runs over, the one named last changes fastest.
Arguments:
- spectra: bfloat16 [192, 20480], P('band'), may hold values from 0 to 3
- theo: bfloat16 [8, 8, 20480], P('query', 'band'), may hold values from -0.0390625 to 0.0390625
- offsets: int32 [16], replicated, may hold values from -128 to 128
- win_lo: int32 [192], P('band'), may hold values from 0 to 32
- win_len: int32 [192], P('band'), may hold values from 1 to 32
Outputs:
- best: float32 [192, 16], P(('band', 'query'))
- average: float32 [192, 16], P(('band', 'query'))
Inputs may be any that keep to these rules, and one draw needn't show every extreme that they name: win_lo + win_len never exceeds 64.
All inputs are finite; a program needn't handle non-finite values.
Results may differ from a plain program's by a relative error of at most 0.003.
Values may be sent and summed in bfloat16 or wider, within the bound.
A program may use at most 128 MiB of HBM per device.

v0:
```python
import jax
import jax.numpy as jnp
from jax import lax
from jax.sharding import PartitionSpec as P

BG_HALF = 75
SHIFT_MAX = 128


def box_table():
    source = lax.broadcasted_iota(jnp.int32, (384, 128), 0)
    target = lax.broadcasted_iota(jnp.int32, (384, 128), 1)
    offset_gap = source - 128 - target
    inside = (jnp.abs(offset_gap) <= BG_HALF) & (offset_gap != 0)
    return inside.astype(jnp.bfloat16)


def correct(intensity):
    row_count, bin_count = intensity.shape
    block_count = bin_count // 128
    blocks = intensity.reshape(row_count, block_count, 128)
    zero_block = jnp.zeros((row_count, 1, 128), intensity.dtype)
    previous = jnp.concatenate([zero_block, blocks[:, :-1]], axis=1)
    following = jnp.concatenate([blocks[:, 1:], zero_block], axis=1)
    stacked = jnp.concatenate([previous, blocks, following], axis=2)
    window_sum = jnp.einsum("rbj,ji->rbi", stacked, box_table(), preferred_element_type=jnp.float32)
    result = blocks.astype(jnp.float32) - window_sum / (2.0 * BG_HALF)
    return result.astype(jnp.bfloat16).reshape(row_count, bin_count)


def shifted_copies(peptides, offsets):
    bin_count = peptides.shape[1]
    padded = jnp.pad(peptides, ((0, 0), (SHIFT_MAX, SHIFT_MAX)))

    def take_shift(offset):
        return lax.dynamic_slice_in_dim(padded, SHIFT_MAX - offset, bin_count, 1)

    copies = jax.vmap(take_shift, out_axes=1)(offsets)
    return copies.reshape(-1, bin_count)


def local(spectra, theo, offsets, win_lo, win_len):
    query_count = lax.axis_size("query")
    spectra_rows = spectra.shape[0]
    own_rows = spectra_rows // query_count
    own_start = lax.axis_index("query") * own_rows
    corrected = correct(spectra)
    shift_count = offsets.shape[0]
    group_size = theo.shape[1] * lax.axis_size("band")
    piece = lax.all_gather(theo, "band", axis=1, tiled=True)
    piece_rows = piece.shape[1]
    copies = shifted_copies(piece[0], offsets)
    partial_scores = jnp.einsum("mb,sb->ms", copies, corrected, preferred_element_type=jnp.float32)
    scores = partial_scores.reshape(1, piece_rows, shift_count * spectra_rows)
    score_table = scores.reshape(group_size, shift_count, query_count, own_rows)
    low_own = lax.dynamic_slice_in_dim(win_lo, own_start, own_rows, 0)
    length_own = lax.dynamic_slice_in_dim(win_len, own_start, own_rows, 0)
    gathered = lax.all_to_all(score_table, "query", split_axis=2, concat_axis=0, tiled=True)
    total_peptides = gathered.shape[0]
    owned_scores = gathered.reshape(total_peptides, shift_count, own_rows)
    peptide_index = lax.broadcasted_iota(jnp.int32, (total_peptides, own_rows), 0)
    inside = (peptide_index >= low_own[None, :]) & (peptide_index < (low_own + length_own)[None, :])
    best_score = jnp.max(jnp.where(inside[:, None, :], owned_scores, -jnp.inf), axis=0).T
    totals = jnp.sum(jnp.where(inside[:, None, :], owned_scores, 0.0), axis=0).T
    average = totals / length_own[:, None].astype(jnp.float32)
    return (best_score, average)


def solution(mesh):
    placed = (P("band", None), P("query", "band", None), P(), P("band"), P("band"))
    return jax.shard_map(
        local,
        mesh=mesh,
        in_specs=placed,
        out_specs=(P(("band", "query"), None), P(("band", "query"), None)),
        check_vma=False,
    )
```

profile of v0, /device:TPU:0, one launch (start us, length us, event | category | flops | bytes accessed | tf_op | source)
XLA Modules:
  0.0 84.9 jit_solution(6701654885838280901)
XLA Ops:
  0.7 1.2 %copy.17 = bf16[1,2,20480]{2,0,1:T(2,128)(2,1)S(1)} copy(bf16[1,2,20480]{2,1,0:T(2,128)(2,1)} %param.6) | data formatting | bytes 163840 | tf_op args[1]
  1.8 12.0 %all_gather.3 = bf16[1,8,20480]{2,0,1:T(2,128)(2,1)S(1)} all-gather(bf16[1,2,20480]{2,0,1:T(2,128)(2,1)S(1)} %copy.17), channel_id=1, replica_groups=mesh['band'=4,'query'=8] {'band'}, dimensions={1}, use_global_device_ids=true | all-gather | bytes 409600 | tf_op jit(solution)/shard_map/all_gather | solution.py:50
  13.8 0.4 copy.28
  14.2 0.7 fusion.29
  14.9 34.0 %while.1 = (s32[]{:T(128)}, bf16[8,20736]{1,0:T(8,128)(2,1)S(1)}, s32[16,2]{0,1:T(2,128)S(1)}, bf16[16,8,20480]{2,1,0:T(8,128)(2,1)}, s32[]{:T(128)}) while((s32[]{:T(128)}, bf16[8,20736]{1,0:T(8,128)(2,1)S(1)}, s32[16,2]{0,1:T(2,128)S(1)}, bf16[16,8,20480]{2,1,0:T(8,128)(2,1)}, s32[]{:T(128)}) %tuple.24), condition=%wide.while_cond, body=%wide.while_body.sunk | while | flops 2 | bytes 655973 | solution.py:36
  14.9 0.1 constant_dynamic-slice_fusion.2
  15.0 0.5 slice.24
  15.5 1.5 %bitcast_dynamic-update-slice_fusion.2 = bf16[16,8,20480]{2,1,0:T(8,128)(2,1)} fusion(bf16[16,8,20480]{2,1,0:T(8,128)(2,1)} %get-tuple-element.58, s32[]{:T(128)S(6)} %copy.32, bf16[8,20736]{1,0:T(8,128)(2,1)S(1)} %get-tuple-element.61, s32[]{:T(128)} %bitcast.41), kind=kLoop, calls=%fused_computation.clone.1 | loop fusion | bytes 655876 | tf_op jit(solution)/shard_map/vmap()/gather
  17.0 0.1 constant_dynamic-slice_fusion.2
  17.1 0.5 slice.24
  17.6 1.5 %bitcast_dynamic-update-slice_fusion.2 = bf16[16,8,20480]{2,1,0:T(8,128)(2,1)} fusion(bf16[16,8,20480]{2,1,0:T(8,128)(2,1)} %get-tuple-element.58, s32[]{:T(128)S(6)} %copy.32, bf16[8,20736]{1,0:T(8,128)(2,1)S(1)} %get-tuple-element.61, s32[]{:T(128)} %bitcast.41), kind=kLoop, calls=%fused_computation.clone.1 | loop fusion | bytes 655876 | tf_op jit(solution)/shard_map/vmap()/gather
  19.2 0.1 constant_dynamic-slice_fusion.2
  19.2 0.5 slice.24
  19.8 1.5 %bitcast_dynamic-update-slice_fusion.2 = bf16[16,8,20480]{2,1,0:T(8,128)(2,1)} fusion(bf16[16,8,20480]{2,1,0:T(8,128)(2,1)} %get-tuple-element.58, s32[]{:T(128)S(6)} %copy.32, bf16[8,20736]{1,0:T(8,128)(2,1)S(1)} %get-tuple-element.61, s32[]{:T(128)} %bitcast.41), kind=kLoop, calls=%fused_computation.clone.1 | loop fusion | bytes 655876 | tf_op jit(solution)/shard_map/vmap()/gather
  21.3 0.1 constant_dynamic-slice_fusion.2
  21.4 0.5 slice.24
  21.9 1.5 %bitcast_dynamic-update-slice_fusion.2 = bf16[16,8,20480]{2,1,0:T(8,128)(2,1)} fusion(bf16[16,8,20480]{2,1,0:T(8,128)(2,1)} %get-tuple-element.58, s32[]{:T(128)S(6)} %copy.32, bf16[8,20736]{1,0:T(8,128)(2,1)S(1)} %get-tuple-element.61, s32[]{:T(128)} %bitcast.41), kind=kLoop, calls=%fused_computation.clone.1 | loop fusion | bytes 655876 | tf_op jit(solution)/shard_map/vmap()/gather
  23.4 0.1 constant_dynamic-slice_fusion.2
  23.5 0.5 slice.24
  24.0 1.5 %bitcast_dynamic-update-slice_fusion.2 = bf16[16,8,20480]{2,1,0:T(8,128)(2,1)} fusion(bf16[16,8,20480]{2,1,0:T(8,128)(2,1)} %get-tuple-element.58, s32[]{:T(128)S(6)} %copy.32, bf16[8,20736]{1,0:T(8,128)(2,1)S(1)} %get-tuple-element.61, s32[]{:T(128)} %bitcast.41), kind=kLoop, calls=%fused_computation.clone.1 | loop fusion | bytes 655876 | tf_op jit(solution)/shard_map/vmap()/gather
  25.5 0.1 constant_dynamic-slice_fusion.2
  25.6 0.5 slice.24
  26.1 1.5 %bitcast_dynamic-update-slice_fusion.2 = bf16[16,8,20480]{2,1,0:T(8,128)(2,1)} fusion(bf16[16,8,20480]{2,1,0:T(8,128)(2,1)} %get-tuple-element.58, s32[]{:T(128)S(6)} %copy.32, bf16[8,20736]{1,0:T(8,128)(2,1)S(1)} %get-tuple-element.61, s32[]{:T(128)} %bitcast.41), kind=kLoop, calls=%fused_computation.clone.1 | loop fusion | bytes 655876 | tf_op jit(solution)/shard_map/vmap()/gather
  27.7 0.1 constant_dynamic-slice_fusion.2
  27.7 0.5 slice.24
  28.2 1.6 %bitcast_dynamic-update-slice_fusion.2 = bf16[16,8,20480]{2,1,0:T(8,128)(2,1)} fusion(bf16[16,8,20480]{2,1,0:T(8,128)(2,1)} %get-tuple-element.58, s32[]{:T(128)S(6)} %copy.32, bf16[8,20736]{1,0:T(8,128)(2,1)S(1)} %get-tuple-element.61, s32[]{:T(128)} %bitcast.41), kind=kLoop, calls=%fused_computation.clone.1 | loop fusion | bytes 655876 | tf_op jit(solution)/shard_map/vmap()/gather
  29.8 0.1 constant_dynamic-slice_fusion.2
  29.9 0.5 slice.24
  30.4 1.5 %bitcast_dynamic-update-slice_fusion.2 = bf16[16,8,20480]{2,1,0:T(8,128)(2,1)} fusion(bf16[16,8,20480]{2,1,0:T(8,128)(2,1)} %get-tuple-element.58, s32[]{:T(128)S(6)} %copy.32, bf16[8,20736]{1,0:T(8,128)(2,1)S(1)} %get-tuple-element.61, s32[]{:T(128)} %bitcast.41), kind=kLoop, calls=%fused_computation.clone.1 | loop fusion | bytes 655876 | tf_op jit(solution)/shard_map/vmap()/gather
  31.9 0.1 constant_dynamic-slice_fusion.2
  32.0 0.5 slice.24
  32.5 1.5 %bitcast_dynamic-update-slice_fusion.2 = bf16[16,8,20480]{2,1,0:T(8,128)(2,1)} fusion(bf16[16,8,20480]{2,1,0:T(8,128)(2,1)} %get-tuple-element.58, s32[]{:T(128)S(6)} %copy.32, bf16[8,20736]{1,0:T(8,128)(2,1)S(1)} %get-tuple-element.61, s32[]{:T(128)} %bitcast.41), kind=kLoop, calls=%fused_computation.clone.1 | loop fusion | bytes 655876 | tf_op jit(solution)/shard_map/vmap()/gather
  34.0 0.1 constant_dynamic-slice_fusion.2
  34.1 0.5 slice.24
  34.6 1.5 %bitcast_dynamic-update-slice_fusion.2 = bf16[16,8,20480]{2,1,0:T(8,128)(2,1)} fusion(bf16[16,8,20480]{2,1,0:T(8,128)(2,1)} %get-tuple-element.58, s32[]{:T(128)S(6)} %copy.32, bf16[8,20736]{1,0:T(8,128)(2,1)S(1)} %get-tuple-element.61, s32[]{:T(128)} %bitcast.41), kind=kLoop, calls=%fused_computation.clone.1 | loop fusion | bytes 655876 | tf_op jit(solution)/shard_map/vmap()/gather
  36.2 0.1 constant_dynamic-slice_fusion.2
  36.2 0.5 slice.24
  36.8 1.5 %bitcast_dynamic-update-slice_fusion.2 = bf16[16,8,20480]{2,1,0:T(8,128)(2,1)} fusion(bf16[16,8,20480]{2,1,0:T(8,128)(2,1)} %get-tuple-element.58, s32[]{:T(128)S(6)} %copy.32, bf16[8,20736]{1,0:T(8,128)(2,1)S(1)} %get-tuple-element.61, s32[]{:T(128)} %bitcast.41), kind=kLoop, calls=%fused_computation.clone.1 | loop fusion | bytes 655876 | tf_op jit(solution)/shard_map/vmap()/gather
  38.4 0.5 slice.24
  38.9 1.5 %bitcast_dynamic-update-slice_fusion.2 = bf16[16,8,20480]{2,1,0:T(8,128)(2,1)} fusion(bf16[16,8,20480]{2,1,0:T(8,128)(2,1)} %get-tuple-element.58, s32[]{:T(128)S(6)} %copy.32, bf16[8,20736]{1,0:T(8,128)(2,1)S(1)} %get-tuple-element.61, s32[]{:T(128)} %bitcast.41), kind=kLoop, calls=%fused_computation.clone.1 | loop fusion | bytes 655876 | tf_op jit(solution)/shard_map/vmap()/gather
  40.5 0.5 slice.24
  41.0 1.5 %bitcast_dynamic-update-slice_fusion.2 = bf16[16,8,20480]{2,1,0:T(8,128)(2,1)} fusion(bf16[16,8,20480]{2,1,0:T(8,128)(2,1)} %get-tuple-element.58, s32[]{:T(128)S(6)} %copy.32, bf16[8,20736]{1,0:T(8,128)(2,1)S(1)} %get-tuple-element.61, s32[]{:T(128)} %bitcast.41), kind=kLoop, calls=%fused_computation.clone.1 | loop fusion | bytes 655876 | tf_op jit(solution)/shard_map/vmap()/gather
  42.6 0.5 slice.24
  43.1 1.5 %bitcast_dynamic-update-slice_fusion.2 = bf16[16,8,20480]{2,1,0:T(8,128)(2,1)} fusion(bf16[16,8,20480]{2,1,0:T(8,128)(2,1)} %get-tuple-element.58, s32[]{:T(128)S(6)} %copy.32, bf16[8,20736]{1,0:T(8,128)(2,1)S(1)} %get-tuple-element.61, s32[]{:T(128)} %bitcast.41), kind=kLoop, calls=%fused_computation.clone.1 | loop fusion | bytes 655876 | tf_op jit(solution)/shard_map/vmap()/gather
  44.7 0.5 slice.24
  45.2 1.5 %bitcast_dynamic-update-slice_fusion.2 = bf16[16,8,20480]{2,1,0:T(8,128)(2,1)} fusion(bf16[16,8,20480]{2,1,0:T(8,128)(2,1)} %get-tuple-element.58, s32[]{:T(128)S(6)} %copy.32, bf16[8,20736]{1,0:T(8,128)(2,1)S(1)} %get-tuple-element.61, s32[]{:T(128)} %bitcast.41), kind=kLoop, calls=%fused_computation.clone.1 | loop fusion | bytes 655876 | tf_op jit(solution)/shard_map/vmap()/gather
  46.8 0.5 slice.24
  47.3 1.5 %bitcast_dynamic-update-slice_fusion.2 = bf16[16,8,20480]{2,1,0:T(8,128)(2,1)} fusion(bf16[16,8,20480]{2,1,0:T(8,128)(2,1)} %get-tuple-element.58, s32[]{:T(128)S(6)} %copy.32, bf16[8,20736]{1,0:T(8,128)(2,1)S(1)} %get-tuple-element.61, s32[]{:T(128)} %bitcast.41), kind=kLoop, calls=%fused_computation.clone.1 | loop fusion | bytes 655876 | tf_op jit(solution)/shard_map/vmap()/gather
  48.9 0.3 copy.22
  49.2 1.2 %fusion.36 = (bf16[48,159,128]{2,1,0:T(8,128)(2,1)S(1)}, bf16[48,159,128]{2,1,0:T(8,128)(2,1)S(1)}) fusion(bf16[48,160,128]{2,1,0:T(8,128)(2,1)S(1)} %bitcast.42), kind=kLoop, calls=%fused_computation.47 | loop fusion | bytes 7815168 | tf_op jit(solution)/shard_map/slice | solution.py:23
  50.4 3.1 %subtract_convert_fusion = bf16[48,160,128]{2,1,0:T(8,128)(2,1)} fusion(bf16[48,160,128]{2,1,0:T(8,128)(2,1)S(1)} %bitcast.43, bf16[48,159,128]{2,1,0:T(8,128)(2,1)S(1)} %get-tuple-element.23, bf16[48,159,128]{2,1,0:T(8,128)(2,1)S(1)} %get-tuple-element.22, s32[384]{0:T(512)S(1)} %iota_add_fusion), kind=kOutput, calls=%fused_computation.16 | convolution fusion | flops 788643840 | bytes 7841280 | tf_op jit(solution)/shard_map/rbj,ji->rbi/dot_general | solution.py:26
  53.5 3.7 %dot_general.9 = bf16[8,6,20480]{2,1,0:T(8,128)(2,1)S(1)} reshape(bf16[48,160,128]{2,1,0:T(8,128)(2,1)} %subtract_convert_fusion) | data formatting | bytes 3932160 | tf_op jit(solution)/shard_map/mb,sb->ms/dot_general | solution.py:53
  57.3 13.3 %fusion.12 = f32[8,16,8,6]{2,0,3,1:T(8,128)S(1)} fusion(bf16[16,8,20480]{2,1,0:T(8,128)(2,1)} %get-tuple-element.9, bf16[8,6,20480]{2,1,0:T(8,128)(2,1)S(1)} %dot_general.9), kind=kOutput, calls=%fused_computation.14 | convolution fusion | flops 251658240 | bytes 7233536 | tf_op jit(solution)/shard_map/mb,sb->ms/dot_general | solution.py:53
  70.6 0.2 copy.19
  70.8 0.7 reshape.74
  71.6 4.9 %all-to-all-start = ((f32[8,1,768]{2,1,0:T(1,128)}), f32[8,1,768]{2,1,0:T(1,128)S(1)}, u32[]{:S(2)}, u32[]{:S(2)}) async-start(f32[8,1,768]{2,1,0:T(1,128)} %reshape.74), calls=%async_computation | async-start | bytes 49152 | tf_op jit(solution)/shard_map/all_to_all | solution.py:58
  76.5 0.1 dynamic-slice_add_fusion
  76.6 0.1 compare_and_fusion
  76.6 5.5 %all-to-all-done = f32[8,1,768]{2,1,0:T(1,128)S(1)} async-done(((f32[8,1,768]{2,1,0:T(1,128)}), f32[8,1,768]{2,1,0:T(1,128)S(1)}, u32[]{:S(2)}, u32[]{:S(2)}) %all-to-all-start) | async-done | bytes 24608 | tf_op jit(solution)/shard_map/all_to_all | solution.py:58
  82.2 0.5 broadcast.91
  82.7 0.7 reduce.2
  83.4 0.1 reshape.75
  83.5 0.7 fusion.20
  84.2 0.7 divide_bitcast_fusion
  (16 shorter events, 0.4 us)
Async XLA Ops:
  0.6 48.3 %copy-start = (bf16[48,20480]{1,0:T(8,128)(2,1)S(1)}, bf16[48,20480]{1,0:T(8,128)(2,1)}, u32[]{:S(2)}) copy-start(bf16[48,20480]{1,0:T(8,128)(2,1)} %param.5) | copy-start | bytes 5898244
  57.2 19.2 %copy-start.1 = (s32[48]{0:T(128)S(1)}, s32[48]{0:T(128)}, u32[]{:S(2)}) copy-start(s32[48]{0:T(128)} %param.9) | copy-start | bytes 580
  57.3 19.2 %copy-start.2 = (s32[48]{0:T(128)S(1)}, s32[48]{0:T(128)}, u32[]{:S(2)}) copy-start(s32[48]{0:T(128)} %param.8) | copy-start | bytes 580
  71.6 10.6 %all-to-all-start = ((f32[8,1,768]{2,1,0:T(1,128)}), f32[8,1,768]{2,1,0:T(1,128)S(1)}, u32[]{:S(2)}, u32[]{:S(2)}) async-start(f32[8,1,768]{2,1,0:T(1,128)} %reshape.74), calls=%async_computation | async-start | bytes 49152 | tf_op jit(solution)/shard_map/all_to_all | solution.py:58
where the time goes:
time: 85.3 us; the launch traced here: 84.9 us
  local copies, waits for them, and re-layouts  42.3 us (50%)
  matrix products  16.4 us (19%)
  blocking collectives  12 us (14%)
  waiting for transfers between devices  5.51 us (6%)
  starting transfers between devices  4.88 us (6%)
  other arithmetic  2.93 us (3%)
    gather x48, local copies, waits for them, and re-layouts  33.9 us
    dot_general x1, matrix products, local(): jnp.einsum('mb,sb->ms', copies, corrected, preferred_element_type=jnp.flo...  13.3 us
    all_gather x1, blocking collectives, local(): piece = lax.all_gather(theo, 'band', axis=1, tiled=True)  12 us
    all_to_all x1, waiting for transfers between devices, local(): lax.all_to_all(score_table, 'query', split_axis=2, concat_axis=0, tiled=T...  5.51 us
    all_to_all x1, starting transfers between devices, local(): lax.all_to_all(score_table, 'query', split_axis=2, concat_axis=0, tiled=T...  4.88 us
    dot_general x2, local copies, waits for them, and re-layouts, local(): jnp.einsum('mb,sb->ms', copies, corrected, preferred_element_type=jnp.flo...  3.95 us
    dot_general x1, matrix products, correct(): jnp.einsum('rbj,ji->rbi', stacked, box_table(), preferred_element_type=jn...  3.08 us
    unnamed x11, local copies, waits for them, and re-layouts  2.71 us
  transfers between devices with their start and end apart: 1, of which 1 were waited for; matrix products, arithmetic and copies ran while one was open for 0% of the time, Pallas kernels for 0%

commit v1 on v0

v1 whole, which is shorter than its diff:
```python
import functools

import jax
import jax.numpy as jnp
from jax import lax
from jax.experimental import pallas as pl
from jax.experimental.pallas import tpu as pltpu
from jax.sharding import PartitionSpec as P

BG_HALF = 75
SHIFT_MAX = 128
LANES = 128
BLOCK = 256
BOX_BLOCKS = 8
STEP = 512
MESH = pl.DeviceIdType.MESH


def box_tables():
    row = lax.broadcasted_iota(jnp.int32, (BLOCK, BLOCK), 0)
    target = lax.broadcasted_iota(jnp.int32, (BLOCK, BLOCK), 1)
    gap = row - target
    middle = (jnp.abs(gap) <= BG_HALF) & (gap != 0)
    side_gap = jnp.where(row < LANES, row - LANES, row + LANES) - target
    side = jnp.abs(side_gap) <= BG_HALF
    return middle.astype(jnp.float32).astype(jnp.bfloat16), side.astype(jnp.float32).astype(jnp.bfloat16)


def column(values, rows):
    row = lax.broadcasted_iota(jnp.int32, (rows, rows), 0)
    lane = lax.broadcasted_iota(jnp.int32, (rows, rows), 1)
    spread = jnp.broadcast_to(values.astype(jnp.float32).reshape(1, rows), (rows, rows))
    return jnp.sum(jnp.where(row == lane, spread, 0.0), axis=1, keepdims=True)


def kernel(
    nb, nq,
    spectra_ref, theo_ref, offsets_ref, lo_ref, len_ref,
    best_ref, average_ref,
    spec, corr, gathered, theo32, tables, send, recv,
    spec_sem, own_sem, band_send, band_recv, query_send, query_recv,
):
    rows, bins = spectra_ref.shape
    peps = theo_ref.shape[1]
    shifts = offsets_ref.shape[0]
    own = rows // nq
    blocks = bins // LANES
    per_chunk = 8 // peps
    chunks = nb * peps // 8
    width = BLOCK * BOX_BLOCKS
    box_steps = bins // width
    band = lax.axis_index("band")
    query = lax.axis_index("query")

    def spec_copy(i):
        start = pl.multiple_of(i * width, width)
        return pltpu.make_async_copy(
            spectra_ref.at[:, pl.ds(start, width)],
            spec.at[:, pl.ds(pl.multiple_of(start + LANES, LANES), width)],
            spec_sem.at[i],
        )

    for i in range(box_steps):
        spec_copy(i).start()
    own_copy = pltpu.make_async_copy(theo_ref.at[0], gathered.at[0], own_sem)
    own_copy.start()

    barrier = pltpu.get_barrier_semaphore()
    for d in range(1, nb):
        pl.semaphore_signal(barrier, inc=1, device_id={"band": lax.rem(band + d, nb)}, device_id_type=MESH)
    for d in range(1, nq):
        pl.semaphore_signal(barrier, inc=1, device_id={"query": lax.rem(query + d, nq)}, device_id_type=MESH)
    pl.semaphore_wait(barrier, nb - 1 + nq - 1)

    def theo_copy(d):
        return pltpu.make_async_remote_copy(
            src_ref=theo_ref.at[0],
            dst_ref=gathered.at[d],
            send_sem=band_send.at[d],
            recv_sem=band_recv.at[d],
            device_id={"band": lax.rem(band + d, nb)},
            device_id_type=MESH,
        )

    for d in range(1, nb):
        theo_copy(d).start()

    spec[:, :LANES] = jnp.zeros((rows, LANES), spec.dtype)
    spec[:, LANES + bins:] = jnp.zeros((rows, LANES), spec.dtype)
    tables[0], tables[1] = box_tables()
    send[...] = jnp.zeros_like(send)
    zero_block = jnp.zeros((8, LANES), jnp.float32)
    for c in range(chunks):
        theo32[c, 0] = zero_block
        theo32[c, blocks + 1] = zero_block
        theo32[c, blocks + 2] = zero_block
    lo = column(lo_ref[...], rows)
    length = column(len_ref[...], rows)
    high = lo + length

    spec_copy(0).wait()

    @pl.loop(0, box_steps)
    def _(i):
        @pl.when(i + 1 < box_steps)
        def _():
            spec_copy(i + 1).wait()

        start = pl.multiple_of(i * width, width)
        middles, sides = [], []
        for j in range(BOX_BLOCKS):
            at = start + j * BLOCK
            before = spec[:, pl.ds(pl.multiple_of(at, LANES), LANES)]
            middles.append(spec[:, pl.ds(pl.multiple_of(at + LANES, LANES), BLOCK)])
            after = spec[:, pl.ds(pl.multiple_of(at + LANES + BLOCK, LANES), LANES)]
            sides.append(jnp.concatenate([before, after], axis=1))
        box = jnp.dot(jnp.concatenate(middles, axis=0), tables[0], preferred_element_type=jnp.float32)
        box += jnp.dot(jnp.concatenate(sides, axis=0), tables[1], preferred_element_type=jnp.float32)
        for j in range(BOX_BLOCKS):
            level = box[j * rows:(j + 1) * rows] * (1.0 / (2.0 * BG_HALF))
            fixed = middles[j].astype(jnp.float32) - level
            corr[:, pl.ds(pl.multiple_of(start + j * BLOCK, BLOCK), BLOCK)] = fixed.astype(jnp.bfloat16)

    own_copy.wait()
    for d in range(1, nb):
        theo_copy(d).wait_recv()

    for c in range(chunks):
        @pl.loop(0, blocks, unroll=4)
        def _(b):
            at = pl.ds(pl.multiple_of(b * LANES, LANES), LANES)
            parts = []
            for j in range(per_chunk):
                slot = lax.rem(band - (c * per_chunk + j) + nb, nb)
                parts.append(gathered[slot, :, at].astype(jnp.float32))
            theo32[c, b + 1] = jnp.concatenate(parts, axis=0)

    lane = lax.broadcasted_iota(jnp.int32, (8, LANES), 1)
    ahead = [SHIFT_MAX - offsets_ref[k] for k in range(shifts)]
    skip = [a // LANES for a in ahead]
    rest = [a % LANES for a in ahead]
    turn = [(LANES - r) % LANES for r in rest]

    wide = shifts * 8
    peptide = lax.broadcasted_iota(jnp.int32, (rows, wide), 1) % 8
    best = jnp.full((rows, wide), -jnp.inf, jnp.float32)
    total = jnp.zeros((rows, wide), jnp.float32)
    for c in range(chunks):
        def step(i, acc):
            first = i * (STEP // LANES)
            columns = []
            for j in range(STEP // LANES):
                parts = []
                for k in range(shifts):
                    near = theo32[c, first + j + skip[k]]
                    far = theo32[c, first + j + skip[k] + 1]
                    parts.append(pltpu.roll(jnp.where(lane < rest[k], far, near), turn[k], 1))
                columns.append(jnp.concatenate(parts, axis=0).astype(jnp.bfloat16))
            shifted = jnp.concatenate(columns, axis=1)
            piece = corr[:, pl.ds(pl.multiple_of(i * STEP, STEP), STEP)]
            return acc + lax.dot_general(
                piece, shifted, (((1,), (1,)), ((), ())), preferred_element_type=jnp.float32
            )

        scores = lax.fori_loop(0, bins // STEP, step, jnp.zeros((rows, wide), jnp.float32))
        number = (peptide + (query * (chunks * 8) + c * 8)).astype(jnp.float32)
        inside = (number >= lo) & (number < high)
        best = jnp.maximum(best, jnp.where(inside, scores, -jnp.inf))
        total = total + jnp.where(inside, scores, 0.0)

    for reach in (4, 2, 1):
        best = jnp.maximum(best, pltpu.roll(best, wide - reach, 1))
        total = total + pltpu.roll(total, wide - reach, 1)
    total = total / length
    spread = lax.broadcasted_iota(jnp.int32, (rows, wide), 1)
    pick = (spread % shifts) * 8
    best = jnp.take_along_axis(best, pick, axis=1)
    total = jnp.take_along_axis(total, pick, axis=1)
    packed = jnp.where(spread < shifts, best, total)
    for q in range(nq):
        send[q, :own] = packed[q * own:(q + 1) * own]

    def result_copy(d):
        return pltpu.make_async_remote_copy(
            src_ref=send.at[lax.rem(query + d, nq)],
            dst_ref=recv.at[d],
            send_sem=query_send.at[d],
            recv_sem=query_recv.at[d],
            device_id={"query": lax.rem(query + d, nq)},
            device_id_type=MESH,
        )

    for d in range(1, nq):
        result_copy(d).start()
    mine = send[query]
    top, mean = mine, mine
    for d in range(1, nq):
        result_copy(d).wait_recv()
        top = jnp.maximum(top, recv[d])
        mean = mean + recv[d]
    best_ref[...] = top[:own, :shifts]
    average_ref[...] = mean[:own, shifts:2 * shifts]
    for d in range(1, nb):
        theo_copy(d).wait_send()
    for d in range(1, nq):
        result_copy(d).wait_send()


def local(spectra, theo, offsets, win_lo, win_len):
    nb, nq = lax.axis_size("band"), lax.axis_size("query")
    rows, bins = spectra.shape
    peps = theo.shape[1]
    shifts = offsets.shape[0]
    own = rows // nq
    slots = (own + 7) // 8 * 8
    chunks = nb * peps // 8
    result = jax.ShapeDtypeStruct((own, shifts), jnp.float32)
    vmem = pl.BlockSpec(memory_space=pltpu.VMEM)
    return pl.pallas_call(
        functools.partial(kernel, nb, nq),
        out_shape=(result, result),
        in_specs=[
            pl.BlockSpec(memory_space=pl.ANY),
            pl.BlockSpec(memory_space=pl.ANY),
            pl.BlockSpec(memory_space=pltpu.SMEM),
            vmem,
            vmem,
        ],
        out_specs=(vmem, vmem),
        scratch_shapes=[
            pltpu.VMEM((rows, bins + 2 * LANES), jnp.bfloat16),
            pltpu.VMEM((rows, bins), jnp.bfloat16),
            pltpu.VMEM((nb, peps, bins), jnp.bfloat16),
            pltpu.VMEM((chunks, bins // LANES + 3, 8, LANES), jnp.float32),
            pltpu.VMEM((2, BLOCK, BLOCK), jnp.bfloat16),
            pltpu.VMEM((nq, slots, LANES), jnp.float32),
            pltpu.VMEM((nq, slots, LANES), jnp.float32),
            pltpu.SemaphoreType.DMA((bins // (BLOCK * BOX_BLOCKS),)),
            pltpu.SemaphoreType.DMA,
            pltpu.SemaphoreType.DMA((nb,)),
            pltpu.SemaphoreType.DMA((nb,)),
            pltpu.SemaphoreType.DMA((nq,)),
            pltpu.SemaphoreType.DMA((nq,)),
        ],
        compiler_params=pltpu.CompilerParams(
            collective_id=0, has_side_effects=True, vmem_limit_bytes=48 * 2**20
        ),
        name="shifted_scores",
    )(spectra, theo, offsets, win_lo, win_len)


def solution(mesh):
    placed = (P("band", None), P("query", "band", None), P(), P("band"), P("band"))
    return jax.shard_map(
        local,
        mesh=mesh,
        in_specs=placed,
        out_specs=(P(("band", "query"), None), P(("band", "query"), None)),
        check_vma=False,
    )
```

time: 85.3 us -> 32.2 us (0.38)
  local copies, waits for them, and re-layouts: 42.3 us -> 5.58 us
  Pallas kernels: 0 us -> 25.8 us
  matrix products: 16.4 us -> 0 us
  blocking collectives: 12 us -> 0 us
  waiting for transfers between devices: 5.51 us -> 0 us
  starting transfers between devices: 4.88 us -> 0 us
  other arithmetic: 2.93 us -> 0 us
    gather x48 -> x0, local copies, waits for them, and re-layouts: 33.9 us -> none
    pallas_call x0 -> x1, Pallas kernels: none -> 25.8 us  [local(): pl.pallas_call(functools.partial(kernel, nb, nq), out_shape=(result, resu...]
    dot_general x2 -> x0, matrix products: 16.4 us -> none  [the longest x1 13.3 us: local(): jnp.einsum('mb,sb->ms', copies, corrected, preferred_element_type=jnp.flo...]
    all_gather x1 -> x0, blocking collectives: 12 us -> none  [local(): piece = lax.all_gather(theo, 'band', axis=1, tiled=True)]
    all_to_all x1 -> x0, waiting for transfers between devices: 5.51 us -> none  [local(): lax.all_to_all(score_table, 'query', split_axis=2, concat_axis=0, tiled=T...]
    all_to_all x1 -> x0, starting transfers between devices: 4.88 us -> none  [local(): lax.all_to_all(score_table, 'query', split_axis=2, concat_axis=0, tiled=T...]
    dot_general x2 -> x0, local copies, waits for them, and re-layouts: 3.95 us -> none  [local(): jnp.einsum('mb,sb->ms', copies, corrected, preferred_element_type=jnp.flo...]
    unnamed x11 -> x12, local copies, waits for them, and re-layouts: 2.71 us -> 5.58 us
  transfers between devices with their start and end apart: 1 -> 0, of which waited for: 1 -> 0; matrix products, arithmetic and copies ran while one was open for 0% -> 0% of each run, Pallas kernels for 0% -> 0%
where the time goes in v1:
time: 32.2 us; the launch traced here: 32 us
  Pallas kernels  25.8 us (80%)
  local copies, waits for them, and re-layouts  5.58 us (17%)
  between operations  0.65 us (2%)
    pallas_call x1, Pallas kernels, local(): pl.pallas_call(functools.partial(kernel, nb, nq), out_shape=(result, resu...  25.8 us
    unnamed x12, local copies, waits for them, and re-layouts  5.58 us

profile of v1, /device:TPU:0, one launch (start us, length us, event | category | flops | bytes accessed | tf_op | source)
XLA Modules:
  0.0 32.0 jit_solution(17569477970012359528)
XLA Ops:
  0.6 0.0 copy-start
  0.6 1.5 %copy-done = bf16[48,20480]{1,0:T(8,128)(2,1)S(1)} copy-done((bf16[48,20480]{1,0:T(8,128)(2,1)S(1)}, bf16[48,20480]{1,0:T(8,128)(2,1)}, u32[]{:S(2)}) %copy-start) | copy-done | bytes 1966104
  2.2 0.0 copy-start.1
  2.2 0.9 %copy-done.1 = bf16[1,2,20480]{2,1,0:T(2,128)(2,1)S(1)} copy-done((bf16[1,2,20480]{2,1,0:T(2,128)(2,1)S(1)}, bf16[1,2,20480]{2,1,0:T(2,128)(2,1)}, u32[]{:S(2)}) %copy-start.1) | copy-done | bytes 81944
  3.1 0.0 copy-start.2
  3.1 0.7 %copy-done.2 = s32[16]{0:T(128)S(1)} copy-done((s32[16]{0:T(128)S(1)}, s32[16]{0:T(128)}, u32[]{:S(2)}) %copy-start.2) | copy-done | bytes 88
  3.7 0.0 copy-start.3
  3.7 0.7 %copy-done.3 = s32[48]{0:T(128)S(1)} copy-done((s32[48]{0:T(128)S(1)}, s32[48]{0:T(128)}, u32[]{:S(2)}) %copy-start.3) | copy-done | bytes 216
  4.4 0.0 copy-start.4
  4.4 0.7 %copy-done.4 = s32[48]{0:T(128)S(1)} copy-done((s32[48]{0:T(128)S(1)}, s32[48]{0:T(128)}, u32[]{:S(2)}) %copy-start.4) | copy-done | bytes 216
  5.0 25.8 %shifted_scores.1 = (f32[6,16]{1,0:T(8,128)S(1)}, f32[6,16]{1,0:T(8,128)S(1)}) custom-call(bf16[48,20480]{1,0:T(8,128)(2,1)S(1)} %copy-done, bf16[1,2,20480]{2,1,0:T(2,128)(2,1)S(1)} %copy-done.1, s32[16]{0:T(128)S(1)} %copy-done.2, s32[48]{0:T(128)S(1)} %copy-done.3, s32[48]{0:T(128)S(1)} %copy-done.4), custom_call_target="tpu_custom_call" | custom-call | tf_op jit(solution)/shard_map/shifted_scores/pallas_call | solution.py:219
  30.8 0.6 %copy.9 = f32[6,16]{1,0:T(8,128)} copy(f32[6,16]{1,0:T(8,128)S(1)} %get-tuple-element.4) | data formatting | bytes 768
  31.4 0.6 %copy.10 = f32[6,16]{1,0:T(8,128)} copy(f32[6,16]{1,0:T(8,128)S(1)} %get-tuple-element.5) | data formatting | bytes 768
Async XLA Ops:
  0.6 1.5 %copy-start = (bf16[48,20480]{1,0:T(8,128)(2,1)S(1)}, bf16[48,20480]{1,0:T(8,128)(2,1)}, u32[]{:S(2)}) copy-start(bf16[48,20480]{1,0:T(8,128)(2,1)} %spectra_ref.1) | copy-start | bytes 5898244
  2.2 0.9 %copy-start.1 = (bf16[1,2,20480]{2,1,0:T(2,128)(2,1)S(1)}, bf16[1,2,20480]{2,1,0:T(2,128)(2,1)}, u32[]{:S(2)}) copy-start(bf16[1,2,20480]{2,1,0:T(2,128)(2,1)} %theo_ref.1) | copy-start | bytes 245764
  3.1 0.7 %copy-start.2 = (s32[16]{0:T(128)S(1)}, s32[16]{0:T(128)}, u32[]{:S(2)}) copy-start(s32[16]{0:T(128)} %offsets_ref.1) | copy-start | bytes 196
  3.7 0.7 %copy-start.3 = (s32[48]{0:T(128)S(1)}, s32[48]{0:T(128)}, u32[]{:S(2)}) copy-start(s32[48]{0:T(128)} %lo_ref.1) | copy-start | bytes 580
  4.4 0.7 %copy-start.4 = (s32[48]{0:T(128)S(1)}, s32[48]{0:T(128)}, u32[]{:S(2)}) copy-start(s32[48]{0:T(128)} %len_ref.1) | copy-start | bytes 580

commit v2 on v1

--- a/solution.py
+++ b/solution.py
@@ -12,7 +12,7 @@
 LANES = 128
 BLOCK = 256
 BOX_BLOCKS = 8
-STEP = 512
+STEP = 2048
 MESH = pl.DeviceIdType.MESH
 
 
@@ -35,14 +35,14 @@
 
 def kernel(
     nb, nq,
-    spectra_ref, theo_ref, offsets_ref, lo_ref, len_ref,
+    spectra_ref, theo_ref, offsets_hbm, lo_hbm, len_hbm,
     best_ref, average_ref,
     spec, corr, gathered, theo32, tables, send, recv,
-    spec_sem, own_sem, band_send, band_recv, query_send, query_recv,
+    offsets_ref, lo_ref, len_ref, small_sem, spec_sem, own_sem, band_send, band_recv, query_send, query_recv,
 ):
     rows, bins = spectra_ref.shape
     peps = theo_ref.shape[1]
-    shifts = offsets_ref.shape[0]
+    shifts = offsets_hbm.shape[0]
     own = rows // nq
     blocks = bins // LANES
     per_chunk = 8 // peps
@@ -64,6 +64,14 @@
         spec_copy(i).start()
     own_copy = pltpu.make_async_copy(theo_ref.at[0], gathered.at[0], own_sem)
     own_copy.start()
+    small = [
+        pltpu.make_async_copy(source, target, small_sem.at[i])
+        for i, (source, target) in enumerate(
+            [(offsets_hbm, offsets_ref), (lo_hbm, lo_ref), (len_hbm, len_ref)]
+        )
+    ]
+    for copy in small:
+        copy.start()
 
     barrier = pltpu.get_barrier_semaphore()
     for d in range(1, nb):
@@ -94,6 +102,8 @@
         theo32[c, 0] = zero_block
         theo32[c, blocks + 1] = zero_block
         theo32[c, blocks + 2] = zero_block
+    for copy in small:
+        copy.wait()
     lo = column(lo_ref[...], rows)
     length = column(len_ref[...], rows)
     high = lo + length
@@ -220,12 +230,8 @@
         functools.partial(kernel, nb, nq),
         out_shape=(result, result),
         in_specs=[
-            pl.BlockSpec(memory_space=pl.ANY),
-            pl.BlockSpec(memory_space=pl.ANY),
-            pl.BlockSpec(memory_space=pltpu.SMEM),
-            vmem,
-            vmem,
-        ],
+            pl.BlockSpec(memory_space=pltpu.HBM),
+        ] * 5,
         out_specs=(vmem, vmem),
         scratch_shapes=[
             pltpu.VMEM((rows, bins + 2 * LANES), jnp.bfloat16),
@@ -235,6 +241,10 @@
             pltpu.VMEM((2, BLOCK, BLOCK), jnp.bfloat16),
             pltpu.VMEM((nq, slots, LANES), jnp.float32),
             pltpu.VMEM((nq, slots, LANES), jnp.float32),
+            pltpu.SMEM((shifts,), jnp.int32),
+            pltpu.VMEM((rows,), jnp.int32),
+            pltpu.VMEM((rows,), jnp.int32),
+            pltpu.SemaphoreType.DMA((3,)),
             pltpu.SemaphoreType.DMA((bins // (BLOCK * BOX_BLOCKS),)),
             pltpu.SemaphoreType.DMA,
             pltpu.SemaphoreType.DMA((nb,)),
@@ -243,7 +253,7 @@
             pltpu.SemaphoreType.DMA((nq,)),
         ],
         compiler_params=pltpu.CompilerParams(
-            collective_id=0, has_side_effects=True, vmem_limit_bytes=48 * 2**20
+            collective_id=0, has_side_effects=True, vmem_limit_bytes=64 * 2**20
         ),
         name="shifted_scores",
     )(spectra, theo, offsets, win_lo, win_len)

time: 32.2 us -> 23.3 us (0.72)
  Pallas kernels: 25.8 us -> 20 us
  local copies, waits for them, and re-layouts: 5.58 us -> 2.53 us
    pallas_call x1, Pallas kernels: 25.8 us -> 20 us  [local(): pl.pallas_call(functools.partial(kernel, nb, nq), out_shape=(result, resu...]
    unnamed x12 -> x2, local copies, waits for them, and re-layouts: 5.58 us -> 2.53 us
where the time goes in v2:
time: 23.3 us; the launch traced here: 23.1 us
  Pallas kernels  20 us (86%)
  local copies, waits for them, and re-layouts  2.53 us (11%)
  between operations  0.64 us (3%)
    pallas_call x1, Pallas kernels, local(): pl.pallas_call(functools.partial(kernel, nb, nq), out_shape=(result, resu...  20 us
    unnamed x2, local copies, waits for them, and re-layouts  2.53 us

profile of v2, /device:TPU:0, one launch (start us, length us, event | category | flops | bytes accessed | tf_op | source)
XLA Modules:
  0.0 23.1 jit_solution(13685413139584200962)
XLA Ops:
  0.6 20.0 %shifted_scores.1 = (f32[6,16]{1,0:T(8,128)}, f32[6,16]{1,0:T(8,128)}) custom-call(bf16[48,20480]{1,0:T(8,128)(2,1)} %spectra_ref.1, bf16[1,2,20480]{2,1,0:T(2,128)(2,1)} %theo_ref.1, s32[16]{0:T(128)} %offsets_hbm.1, s32[48]{0:T(128)} %lo_hbm.1, s32[48]{0:T(128)} %len_hbm.1), custom_call_target="tpu_custom_call" | custom-call | tf_op jit(solution)/shard_map/shifted_scores/pallas_call | solution.py:229
  20.6 1.3 %copy.9 = f32[6,16]{1,0:T(8,128)} copy(f32[6,16]{1,0:T(8,128)} %get-tuple-element.4) | data formatting | bytes 768
  21.9 1.3 %copy.10 = f32[6,16]{1,0:T(8,128)} copy(f32[6,16]{1,0:T(8,128)} %get-tuple-element.5) | data formatting | bytes 768

commit v3 on v2

--- a/solution.py
+++ b/solution.py
@@ -13,6 +13,7 @@
 BLOCK = 256
 BOX_BLOCKS = 8
 STEP = 2048
+PARTS = 2
 MESH = pl.DeviceIdType.MESH
 
 
@@ -36,8 +37,8 @@
 def kernel(
     nb, nq,
     spectra_ref, theo_ref, offsets_hbm, lo_hbm, len_hbm,
-    best_ref, average_ref,
-    spec, corr, gathered, theo32, tables, send, recv,
+    out_ref,
+    spec, corr, gathered, pairs, tables, send, recv,
     offsets_ref, lo_ref, len_ref, small_sem, spec_sem, own_sem, band_send, band_recv, query_send, query_recv,
 ):
     rows, bins = spectra_ref.shape
@@ -62,7 +63,7 @@
 
     for i in range(box_steps):
         spec_copy(i).start()
-    own_copy = pltpu.make_async_copy(theo_ref.at[0], gathered.at[0], own_sem)
+    own_copy = pltpu.make_async_copy(theo_ref.at[0], gathered.at[0, :, pl.ds(0, bins)], own_sem)
     own_copy.start()
     small = [
         pltpu.make_async_copy(source, target, small_sem.at[i])
@@ -80,28 +81,29 @@
         pl.semaphore_signal(barrier, inc=1, device_id={"query": lax.rem(query + d, nq)}, device_id_type=MESH)
     pl.semaphore_wait(barrier, nb - 1 + nq - 1)
 
-    def theo_copy(d):
+    part = bins // PARTS
+
+    def theo_copy(d, h):
         return pltpu.make_async_remote_copy(
-            src_ref=theo_ref.at[0],
-            dst_ref=gathered.at[d],
-            send_sem=band_send.at[d],
-            recv_sem=band_recv.at[d],
+            src_ref=theo_ref.at[0, :, pl.ds(h * part, part)],
+            dst_ref=gathered.at[d, :, pl.ds(h * part, part)],
+            send_sem=band_send.at[d, h],
+            recv_sem=band_recv.at[d, h],
             device_id={"band": lax.rem(band + d, nb)},
             device_id_type=MESH,
         )
 
-    for d in range(1, nb):
-        theo_copy(d).start()
+    for h in range(PARTS):
+        for d in range(1, nb):
+            theo_copy(d, h).start()
 
     spec[:, :LANES] = jnp.zeros((rows, LANES), spec.dtype)
     spec[:, LANES + bins:] = jnp.zeros((rows, LANES), spec.dtype)
     tables[0], tables[1] = box_tables()
     send[...] = jnp.zeros_like(send)
-    zero_block = jnp.zeros((8, LANES), jnp.float32)
+    gathered[:, :, bins:] = jnp.zeros((nb, peps, LANES), gathered.dtype)
     for c in range(chunks):
-        theo32[c, 0] = zero_block
-        theo32[c, blocks + 1] = zero_block
-        theo32[c, blocks + 2] = zero_block
+        pairs[c, blocks + 1] = jnp.zeros((16, LANES), pairs.dtype)
     for copy in small:
         copy.wait()
     lo = column(lo_ref[...], rows)
@@ -132,49 +134,76 @@
             corr[:, pl.ds(pl.multiple_of(start + j * BLOCK, BLOCK), BLOCK)] = fixed.astype(jnp.bfloat16)
 
     own_copy.wait()
-    for d in range(1, nb):
-        theo_copy(d).wait_recv()
-
-    for c in range(chunks):
-        @pl.loop(0, blocks, unroll=4)
-        def _(b):
-            at = pl.ds(pl.multiple_of(b * LANES, LANES), LANES)
-            parts = []
-            for j in range(per_chunk):
-                slot = lax.rem(band - (c * per_chunk + j) + nb, nb)
-                parts.append(gathered[slot, :, at].astype(jnp.float32))
-            theo32[c, b + 1] = jnp.concatenate(parts, axis=0)
-
-    lane = lax.broadcasted_iota(jnp.int32, (8, LANES), 1)
+    lane = lax.broadcasted_iota(jnp.int32, (16, LANES), 1).astype(jnp.float32).astype(jnp.bfloat16)
     ahead = [SHIFT_MAX - offsets_ref[k] for k in range(shifts)]
     skip = [a // LANES for a in ahead]
     rest = [a % LANES for a in ahead]
     turn = [(LANES - r) % LANES for r in rest]
-
-    wide = shifts * 8
-    peptide = lax.broadcasted_iota(jnp.int32, (rows, wide), 1) % 8
+    edge = [jnp.full((16, LANES), r.astype(jnp.float32)).astype(jnp.bfloat16) for r in rest]
+    per_step = STEP // LANES
+    wide = shifts * 16
+
+    def read_blocks(c, first):
+        at = pl.ds(pl.multiple_of(first * LANES, LANES), 9 * LANES)
+        rows_of = []
+        for j in range(per_chunk):
+            slot = lax.rem(band - (c * per_chunk + j) + nb, nb)
+            rows_of.append(gathered[slot, :, at].astype(jnp.float32))
+        whole = jnp.concatenate(rows_of, axis=0)
+        return [whole[:, t * LANES:(t + 1) * LANES] for t in range(9)]
+
+    def pair(c, g):
+        found = read_blocks(c, g * 8)
+        for t in range(8):
+            pairs[c, g * 8 + t + 1] = jnp.concatenate(found[t:t + 2], axis=0).astype(jnp.bfloat16)
+
+    def step(c, i, acc):
+        first = i * per_step
+        columns, evens, odds = [], [], []
+        for j in range(0, per_step, 2):
+            parts = []
+            for k in range(shifts):
+                near = pairs[c, first + j + skip[k]]
+                far = pairs[c, first + j + skip[k] + 1]
+                parts.append(pltpu.roll(jnp.where(lane < edge[k], far, near), turn[k], 1))
+            columns.append(jnp.concatenate(parts, axis=0))
+            at = (first + j) * LANES
+            evens.append(corr[:, pl.ds(pl.multiple_of(at, LANES), LANES)])
+            odds.append(corr[:, pl.ds(pl.multiple_of(at + LANES, LANES), LANES)])
+        shifted = jnp.concatenate(columns, axis=1)
+        piece = jnp.concatenate(
+            [jnp.concatenate(evens, axis=1), jnp.concatenate(odds, axis=1)], axis=0
+        )
+        return acc + lax.dot_general(
+            piece, shifted, (((1,), (1,)), ((), ())), preferred_element_type=jnp.float32
+        )
+
+    sums = [jnp.zeros((2 * rows, wide), jnp.float32)] * chunks
+    group_from = step_from = 0
+    for h in range(PARTS):
+        for d in range(1, nb):
+            theo_copy(d, h).wait_recv()
+        if h < PARTS - 1:
+            group_to = ((h + 1) * part // LANES - 1) // 8
+            step_to = (group_to * 8 - per_step - 1) // per_step + 1
+        else:
+            group_to, step_to = blocks // 8, bins // STEP
+        for c in range(chunks):
+            if h == 0:
+                start = read_blocks(c, 0)[0]
+                pairs[c, 0] = jnp.concatenate([jnp.zeros_like(start), start], axis=0).astype(jnp.bfloat16)
+            pl.loop(group_from, group_to)(functools.partial(pair, c))
+            sums[c] = lax.fori_loop(step_from, step_to, functools.partial(step, c), sums[c])
+        group_from, step_from = group_to, step_to
+
+    spread = lax.broadcasted_iota(jnp.int32, (rows, wide), 1)
+    peptide = spread % 16
     best = jnp.full((rows, wide), -jnp.inf, jnp.float32)
     total = jnp.zeros((rows, wide), jnp.float32)
     for c in range(chunks):
-        def step(i, acc):
-            first = i * (STEP // LANES)
-            columns = []
-            for j in range(STEP // LANES):
-                parts = []
-                for k in range(shifts):
-                    near = theo32[c, first + j + skip[k]]
-                    far = theo32[c, first + j + skip[k] + 1]
-                    parts.append(pltpu.roll(jnp.where(lane < rest[k], far, near), turn[k], 1))
-                columns.append(jnp.concatenate(parts, axis=0).astype(jnp.bfloat16))
-            shifted = jnp.concatenate(columns, axis=1)
-            piece = corr[:, pl.ds(pl.multiple_of(i * STEP, STEP), STEP)]
-            return acc + lax.dot_general(
-                piece, shifted, (((1,), (1,)), ((), ())), preferred_element_type=jnp.float32
-            )
-
-        scores = lax.fori_loop(0, bins // STEP, step, jnp.zeros((rows, wide), jnp.float32))
+        scores = sums[c][:rows] + pltpu.roll(sums[c][rows:], wide - 8, 1)
         number = (peptide + (query * (chunks * 8) + c * 8)).astype(jnp.float32)
-        inside = (number >= lo) & (number < high)
+        inside = (peptide < 8) & (number >= lo) & (number < high)
         best = jnp.maximum(best, jnp.where(inside, scores, -jnp.inf))
         total = total + jnp.where(inside, scores, 0.0)
 
@@ -182,11 +211,14 @@
         best = jnp.maximum(best, pltpu.roll(best, wide - reach, 1))
         total = total + pltpu.roll(total, wide - reach, 1)
     total = total / length
-    spread = lax.broadcasted_iota(jnp.int32, (rows, wide), 1)
-    pick = (spread % shifts) * 8
-    best = jnp.take_along_axis(best, pick, axis=1)
-    total = jnp.take_along_axis(total, pick, axis=1)
-    packed = jnp.where(spread < shifts, best, total)
+    spread = lax.broadcasted_iota(jnp.int32, (rows, LANES), 1)
+    pick = (spread % 8) * 16
+    packed = jnp.zeros((rows, LANES), jnp.float32)
+    for n, source in enumerate((best, total)):
+        for v in range(wide // LANES):
+            place = n * shifts + v * 8
+            taken = jnp.take_along_axis(source[:, v * LANES:(v + 1) * LANES], pick, axis=1)
+            packed = jnp.where((spread >= place) & (spread < place + 8), taken, packed)
     for q in range(nq):
         send[q, :own] = packed[q * own:(q + 1) * own]
 
@@ -208,10 +240,11 @@
         result_copy(d).wait_recv()
         top = jnp.maximum(top, recv[d])
         mean = mean + recv[d]
-    best_ref[...] = top[:own, :shifts]
-    average_ref[...] = mean[:own, shifts:2 * shifts]
-    for d in range(1, nb):
-        theo_copy(d).wait_send()
+    place = lax.broadcasted_iota(jnp.int32, top.shape, 1)
+    out_ref[...] = jnp.where(place < shifts, top, mean)[:own, :2 * shifts]
+    for h in range(PARTS):
+        for d in range(1, nb):
+            theo_copy(d, h).wait_send()
     for d in range(1, nq):
         result_copy(d).wait_send()
 
@@ -224,20 +257,20 @@
     own = rows // nq
     slots = (own + 7) // 8 * 8
     chunks = nb * peps // 8
-    result = jax.ShapeDtypeStruct((own, shifts), jnp.float32)
+    result = jax.ShapeDtypeStruct((own, 2 * shifts), jnp.float32)
     vmem = pl.BlockSpec(memory_space=pltpu.VMEM)
-    return pl.pallas_call(
+    both = pl.pallas_call(
         functools.partial(kernel, nb, nq),
-        out_shape=(result, result),
+        out_shape=result,
         in_specs=[
             pl.BlockSpec(memory_space=pltpu.HBM),
         ] * 5,
-        out_specs=(vmem, vmem),
+        out_specs=vmem,
         scratch_shapes=[
             pltpu.VMEM((rows, bins + 2 * LANES), jnp.bfloat16),
             pltpu.VMEM((rows, bins), jnp.bfloat16),
-            pltpu.VMEM((nb, peps, bins), jnp.bfloat16),
-            pltpu.VMEM((chunks, bins // LANES + 3, 8, LANES), jnp.float32),
+            pltpu.VMEM((nb, peps, bins + LANES), jnp.bfloat16),
+            pltpu.VMEM((chunks, bins // LANES + 2, 16, LANES), jnp.bfloat16),
             pltpu.VMEM((2, BLOCK, BLOCK), jnp.bfloat16),
             pltpu.VMEM((nq, slots, LANES), jnp.float32),
             pltpu.VMEM((nq, slots, LANES), jnp.float32),
@@ -247,8 +280,8 @@
             pltpu.SemaphoreType.DMA((3,)),
             pltpu.SemaphoreType.DMA((bins // (BLOCK * BOX_BLOCKS),)),
             pltpu.SemaphoreType.DMA,
-            pltpu.SemaphoreType.DMA((nb,)),
-            pltpu.SemaphoreType.DMA((nb,)),
+            pltpu.SemaphoreType.DMA((nb, PARTS)),
+            pltpu.SemaphoreType.DMA((nb, PARTS)),
             pltpu.SemaphoreType.DMA((nq,)),
             pltpu.SemaphoreType.DMA((nq,)),
         ],
@@ -257,6 +290,7 @@
         ),
         name="shifted_scores",
     )(spectra, theo, offsets, win_lo, win_len)
+    return both[:, :shifts], both[:, shifts:]
 
 
 def solution(mesh):

time: 23.3 us -> 20.8 us (0.89)
  Pallas kernels: 20 us -> 18.5 us
  local copies, waits for them, and re-layouts: 2.53 us -> 1.41 us
    unnamed x2 -> x0, local copies, waits for them, and re-layouts: 2.53 us -> none
    pallas_call x1, Pallas kernels: 20 us -> 18.5 us  [local(): pl.pallas_call(functools.partial(kernel, nb, nq), out_shape=result, in_sp...]
    slice x0 -> x1, local copies, waits for them, and re-layouts: none -> 1.41 us  [local(): return (both[:, :shifts], both[:, shifts:])]
where the time goes in v3:
time: 20.8 us; the launch traced here: 20.6 us
  Pallas kernels  18.5 us (89%)
  local copies, waits for them, and re-layouts  1.41 us (7%)
  between operations  0.64 us (3%)
    pallas_call x1, Pallas kernels, local(): pl.pallas_call(functools.partial(kernel, nb, nq), out_shape=result, in_sp...  18.5 us
    slice x1, local copies, waits for them, and re-layouts, local(): return (both[:, :shifts], both[:, shifts:])  1.41 us

profile of v3, /device:TPU:0, one launch (start us, length us, event | category | flops | bytes accessed | tf_op | source)
XLA Modules:
  0.0 20.6 jit_solution(9418889341536998837)
XLA Ops:
  0.6 18.5 %shifted_scores.1 = f32[6,32]{1,0:T(8,128)} custom-call(bf16[48,20480]{1,0:T(8,128)(2,1)} %spectra_ref.1, bf16[1,2,20480]{2,1,0:T(2,128)(2,1)} %theo_ref.1, s32[16]{0:T(128)} %offsets_hbm.1, s32[48]{0:T(128)} %lo_hbm.1, s32[48]{0:T(128)} %len_hbm.1), custom_call_target="tpu_custom_call" | custom-call | tf_op jit(solution)/shard_map/shifted_scores/pallas_call | solution.py:262
  19.2 1.4 %fusion = (f32[6,16]{1,0:T(8,128)}, f32[6,16]{1,0:T(8,128)}) fusion(f32[6,32]{1,0:T(8,128)} %shifted_scores.1), kind=kLoop, calls=%fused_computation | loop fusion | bytes 1536 | tf_op jit(solution)/shard_map/slice | solution.py:293

commit v4 on v3

--- a/solution.py
+++ b/solution.py
@@ -11,8 +11,8 @@
 SHIFT_MAX = 128
 LANES = 128
 BLOCK = 256
-BOX_BLOCKS = 8
-STEP = 2048
+BOX_BLOCKS = 16
+STEP = 4096
 PARTS = 2
 MESH = pl.DeviceIdType.MESH
 
@@ -53,6 +53,12 @@
     band = lax.axis_index("band")
     query = lax.axis_index("query")
 
+    barrier = pltpu.get_barrier_semaphore()
+    for d in range(1, nb):
+        pl.semaphore_signal(barrier, inc=1, device_id={"band": lax.rem(band + d, nb)}, device_id_type=MESH)
+    for d in range(1, nq):
+        pl.semaphore_signal(barrier, inc=1, device_id={"query": lax.rem(query + d, nq)}, device_id_type=MESH)
+
     def spec_copy(i):
         start = pl.multiple_of(i * width, width)
         return pltpu.make_async_copy(
@@ -74,11 +80,6 @@
     for copy in small:
         copy.start()
 
-    barrier = pltpu.get_barrier_semaphore()
-    for d in range(1, nb):
-        pl.semaphore_signal(barrier, inc=1, device_id={"band": lax.rem(band + d, nb)}, device_id_type=MESH)
-    for d in range(1, nq):
-        pl.semaphore_signal(barrier, inc=1, device_id={"query": lax.rem(query + d, nq)}, device_id_type=MESH)
     pl.semaphore_wait(barrier, nb - 1 + nq - 1)
 
     part = bins // PARTS
@@ -192,7 +193,7 @@
             if h == 0:
                 start = read_blocks(c, 0)[0]
                 pairs[c, 0] = jnp.concatenate([jnp.zeros_like(start), start], axis=0).astype(jnp.bfloat16)
-            pl.loop(group_from, group_to)(functools.partial(pair, c))
+            pl.loop(group_from, group_to, unroll=True)(functools.partial(pair, c))
             sums[c] = lax.fori_loop(step_from, step_to, functools.partial(step, c), sums[c])
         group_from, step_from = group_to, step_to
 
@@ -240,8 +241,8 @@
         result_copy(d).wait_recv()
         top = jnp.maximum(top, recv[d])
         mean = mean + recv[d]
-    place = lax.broadcasted_iota(jnp.int32, top.shape, 1)
-    out_ref[...] = jnp.where(place < shifts, top, mean)[:own, :2 * shifts]
+    out_ref[0] = top[:own, :shifts]
+    out_ref[1] = pltpu.roll(mean, LANES - shifts, 1)[:own, :shifts]
     for h in range(PARTS):
         for d in range(1, nb):
             theo_copy(d, h).wait_send()
@@ -257,7 +258,7 @@
     own = rows // nq
     slots = (own + 7) // 8 * 8
     chunks = nb * peps // 8
-    result = jax.ShapeDtypeStruct((own, 2 * shifts), jnp.float32)
+    result = jax.ShapeDtypeStruct((2, own, shifts), jnp.float32)
     vmem = pl.BlockSpec(memory_space=pltpu.VMEM)
     both = pl.pallas_call(
         functools.partial(kernel, nb, nq),
@@ -290,7 +291,7 @@
         ),
         name="shifted_scores",
     )(spectra, theo, offsets, win_lo, win_len)
-    return both[:, :shifts], both[:, shifts:]
+    return both[0], both[1]
 
 
 def solution(mesh):

time: 20.8 us -> 19.6 us (0.942)
  Pallas kernels: 18.5 us -> 17.5 us
    slice x1 -> x0, local copies, waits for them, and re-layouts: 1.41 us -> none  [local(): return (both[:, :shifts], both[:, shifts:])]
    squeeze x0 -> x1, local copies, waits for them, and re-layouts: none -> 1.28 us  [local(): return (both[0], both[1])]
    pallas_call x1, Pallas kernels: 18.5 us -> 17.5 us  [local(): pl.pallas_call(functools.partial(kernel, nb, nq), out_shape=result, in_sp...]
where the time goes in v4:
time: 19.6 us; the launch traced here: 19.4 us
  Pallas kernels  17.5 us (89%)
  local copies, waits for them, and re-layouts  1.28 us (7%)
  between operations  0.64 us (3%)
    pallas_call x1, Pallas kernels, local(): pl.pallas_call(functools.partial(kernel, nb, nq), out_shape=result, in_sp...  17.5 us
    squeeze x1, local copies, waits for them, and re-layouts, local(): return (both[0], both[1])  1.28 us

profile of v4, /device:TPU:0, one launch (start us, length us, event | category | flops | bytes accessed | tf_op | source)
XLA Modules:
  0.0 19.4 jit_solution(7267003968176820496)
XLA Ops:
  0.6 17.5 %shifted_scores.1 = f32[2,6,16]{2,1,0:T(8,128)} custom-call(bf16[48,20480]{1,0:T(8,128)(2,1)} %spectra_ref.1, bf16[1,2,20480]{2,1,0:T(2,128)(2,1)} %theo_ref.1, s32[16]{0:T(128)} %offsets_hbm.1, s32[48]{0:T(128)} %lo_hbm.1, s32[48]{0:T(128)} %len_hbm.1), custom_call_target="tpu_custom_call" | custom-call | tf_op jit(solution)/shard_map/shifted_scores/pallas_call | solution.py:263
  18.1 1.3 %slice_bitcast_fusion = (f32[6,16]{1,0:T(8,128)}, f32[6,16]{1,0:T(8,128)}) fusion(f32[2,6,16]{2,1,0:T(8,128)} %shifted_scores.1), kind=kLoop, calls=%fused_computation | loop fusion | bytes 1536 | tf_op jit(solution)/shard_map/squeeze | solution.py:294

commit v5 on v4

--- a/solution.py
+++ b/solution.py
@@ -95,7 +95,7 @@
         )
 
     for h in range(PARTS):
-        for d in range(1, nb):
+        for d in sorted(range(1, nb), key=lambda d: abs(d - nb // 2)):
             theo_copy(d, h).start()
 
     spec[:, :LANES] = jnp.zeros((rows, LANES), spec.dtype)

time: 19.6 us -> 19.6 us (level)
  no operation moved by 1% of the time
where the time goes in v5:
time: 19.6 us; the launch traced here: 19.4 us
  Pallas kernels  17.5 us (89%)
  local copies, waits for them, and re-layouts  1.28 us (7%)
  between operations  0.64 us (3%)
    pallas_call x1, Pallas kernels, local(): pl.pallas_call(functools.partial(kernel, nb, nq), out_shape=result, in_sp...  17.5 us
    squeeze x1, local copies, waits for them, and re-layouts, local(): return (both[0], both[1])  1.28 us

profile of v5, /device:TPU:0, one launch (start us, length us, event | category | flops | bytes accessed | tf_op | source)
XLA Modules:
  0.0 19.4 jit_solution(3846179428146754853)
XLA Ops:
  0.6 17.5 %shifted_scores.1 = f32[2,6,16]{2,1,0:T(8,128)} custom-call(bf16[48,20480]{1,0:T(8,128)(2,1)} %spectra_ref.1, bf16[1,2,20480]{2,1,0:T(2,128)(2,1)} %theo_ref.1, s32[16]{0:T(128)} %offsets_hbm.1, s32[48]{0:T(128)} %lo_hbm.1, s32[48]{0:T(128)} %len_hbm.1), custom_call_target="tpu_custom_call" | custom-call | tf_op jit(solution)/shard_map/shifted_scores/pallas_call | solution.py:263
  18.1 1.3 %slice_bitcast_fusion = (f32[6,16]{1,0:T(8,128)}, f32[6,16]{1,0:T(8,128)}) fusion(f32[2,6,16]{2,1,0:T(8,128)} %shifted_scores.1), kind=kLoop, calls=%fused_computation | loop fusion | bytes 1536 | tf_op jit(solution)/shard_map/squeeze | solution.py:294
